TPU v7x, 256 devices: a whole 4x4x8 slice. The times are simulated.
256 devices in a mesh: row: 16 (over y, x_hi, core), col: 16 (over z, x_lo).
Axes of the slice: x: 4 (x_hi: 2, x_lo: 2; x = x_hi * 2 + x_lo), y: 4, z: 8, core: 2. Of those that a mesh axis runs over, the one named last changes fastest.
Arguments:
- cell_batch: bfloat16 [2048, 20480], P('col', 'row'), may hold values from -6 to 6
- cov_prior: bfloat16 [20480, 20480], P('row', 'col'), as said below
- omega_prior: bfloat16 [20480, 20480], P('row', 'col'), as said below
Outputs:
- cov_updated: bfloat16 [20480, 20480], P('row', 'col')
- omega_panel: bfloat16 [1024, 20480], P('col', 'row')
- column_objective: float32 [1024], P('col')
Inputs may be any that keep to these rules, and one draw needn't show every extreme that they name: `cov_prior`: Symmetric; its diagonal entries lie between 0.5 and 1.5. `omega_prior`: Symmetric; its diagonal entries lie between 1 and 4.
All inputs are finite; a program needn't handle non-finite values.
Results may differ from a plain program's by a relative error of at most 0.0047.
Values may be sent and summed in bfloat16 or wider, within the bound.
A program may use at most 128 MiB of HBM per device.

v0:
```python
import jax
import jax.numpy as jnp
from jax import lax
from jax.sharding import PartitionSpec as P

P_SIZE = 20480
PW = 64
decay_weight = 0.5
step_size = 0.2
penalty = 1.0


def broadcast(value, axis, source):
    kept = jnp.where(lax.axis_index(axis) == source, value, 0).astype(value.dtype)
    return lax.psum(kept, axis)


def contract(left_rows, right_rows):
    return lax.dot_general(
        left_rows, right_rows, (((1,), (1,)), ((), ())), preferred_element_type=jnp.float32
    )


def per_device(cell_batch, cov_prior, omega_prior):
    rows_count = lax.axis_size("row")
    cols_count = lax.axis_size("col")
    fold_ratio = rows_count // cols_count
    row_width = omega_prior.shape[0]
    col_number = lax.axis_index("col")
    row_number = lax.axis_index("row")
    own_slab = lax.all_gather(cell_batch, "col", axis=0, tiled=True)
    mirrored = broadcast(own_slab, "row", col_number * fold_ratio + 0)
    product = lax.dot_general(
        own_slab, mirrored, (((0,), (0,)), ((), ())), preferred_element_type=jnp.float32
    )
    scale_new = (1.0 - decay_weight) / own_slab.shape[0]
    cov_updated = (decay_weight * cov_prior.astype(jnp.float32) + scale_new * product).astype(
        jnp.bfloat16
    )
    cov_rows, omega_rows = (
        lax.all_gather(cov_updated[:PW], "row", axis=0, tiled=True),
        lax.all_gather(omega_prior[:PW], "row", axis=0, tiled=True),
    )
    own_rows = PW * fold_ratio
    omega_cols_half = (
        omega_prior.reshape(row_width, fold_ratio, row_width)[:, :, :PW]
        .reshape(row_width, own_rows)
        .T
    )
    omega_vals = omega_cols_half.astype(jnp.float32)
    positions = lax.iota(jnp.int32, own_rows)
    same_block = row_number == col_number * fold_ratio + positions // PW
    diagonal = same_block[:, None] & (
        (positions % PW)[:, None] == lax.iota(jnp.int32, row_width)[None, :]
    )
    own_diag = jnp.where(diagonal, omega_vals, jnp.float32(1.0))
    inverse = jnp.where(diagonal, 1.0 / own_diag, jnp.float32(0.0))
    logs = jnp.sum(jnp.where(diagonal, jnp.log(own_diag), jnp.float32(0.0)), axis=1)
    lasso = penalty * jnp.sum(jnp.where(diagonal, jnp.float32(0.0), jnp.abs(omega_vals)), axis=1)
    summed = lax.psum_scatter(
        jnp.concatenate(
            [contract(cov_rows, omega_prior), contract(omega_rows, cov_updated)], axis=1
        ),
        "col",
        scatter_dimension=0,
        tiled=True,
    )
    first_sum = summed[:, :row_width]
    second_sum = summed[:, row_width:]
    both_sum = first_sum + second_sum
    quadratic = 0.5 * jnp.sum(omega_vals * second_sum, axis=1)
    column_objective = lax.psum(quadratic + lasso - logs, "row") / P_SIZE
    gradient = 0.5 * both_sum - inverse
    stepped = omega_vals - step_size * gradient
    shrunk = jnp.sign(stepped) * jnp.maximum(jnp.abs(stepped) - step_size * penalty, 0.0)
    omega_panel = jnp.where(diagonal, stepped, shrunk).astype(jnp.bfloat16)
    return (cov_updated, omega_panel, column_objective)


def solution(mesh):
    return jax.shard_map(
        per_device,
        mesh=mesh,
        in_specs=(P("col", "row"), P("row", "col"), P("row", "col")),
        out_specs=(P("row", "col"), P("col", "row"), P("col")),
        check_vma=False,
    )
```

profile of v0, /device:TPU:32, one launch (start us, length us, event | category | flops | bytes accessed | tf_op | source)
XLA Modules:
  0.0 705.4 jit_solution(16349236336308614956)
XLA Ops:
  7.2 0.0 all-gather.4.cloned.1.call-start
  7.2 0.7 all-gather.4.cloned.1.call-update
  7.9 0.0 all-reduce.2.cloned.1.call-start
  8.0 123.7 %all-gather.4.cloned.1.call-done = bf16[2048,1280]{1,0:T(8,128)(2,1)} async-done(((bf16[128,1280]{1,0:T(8,128)(2,1)}), bf16[2048,1280]{1,0:T(8,128)(2,1)}) %all-gather.4.cloned.1.call-update) | async-done | bytes 5242896 | tf_op jit(solution)/shard_map/all_gather | solution.py:31
  131.6 2.7 broadcast_select_fusion
  134.3 0.0 copy-start
  134.3 0.0 all-reduce.2.cloned.1.call-update
  134.3 0.0 all-gather.8.cloned.1.call-start
  134.4 1.9 copy-done
  136.2 0.7 slice.17
  136.9 0.0 all-gather.8.cloned.1.call-update
  136.9 0.0 all-gather.6.cloned.1.call-start
  137.0 167.5 %all-reduce.2.cloned.1.call-done = bf16[2048,1280]{1,0:T(8,128)(2,1)} async-done(((bf16[2048,1280]{1,0:T(8,128)(2,1)}), bf16[2048,1280]{1,0:T(8,128)(2,1)}) %all-reduce.2.cloned.1.call-update) | async-done | bytes 5242896 | tf_op jit(solution)/shard_map/psum | solution.py:15
  304.5 11.3 %fusion.2 = bf16[1280,1280]{1,0:T(8,128)(2,1)S(1)} fusion(bf16[2048,1280]{1,0:T(8,128)(2,1)} %all-reduce.2.cloned.1.call-done, bf16[2048,1280]{1,0:T(8,128)(2,1)} %all-gather.4.cloned.1.call-done, bf16[1280,1280]{1,0:T(8,128)(2,1)} %param.4), kind=kOutput, calls=%fused_computation.4 | convolution fusion | flops 6719078400 | bytes 17039360 | tf_op jit(solution)/shard_map/dot_general | solution.py:33
  315.8 0.0 copy-start.1
  315.8 1.7 copy-done.1
  317.5 0.7 slice.21
  318.2 0.0 all-gather.6.cloned.1.call-update
  318.2 0.0 reduce-scatter.2.cloned.1.call-start
  318.2 43.7 %all-gather.8.cloned.1.call-done = bf16[1024,1280]{1,0:T(8,128)(2,1)} async-done(((bf16[64,1280]{1,0:T(8,128)(2,1)}), bf16[1024,1280]{1,0:T(8,128)(2,1)}) %all-gather.8.cloned.1.call-update) | async-done | bytes 2621456 | tf_op jit(solution)/shard_map/all_gather | solution.py:42
  362.0 8.7 %convolution_bitcast_fusion = f32[1024,1280]{1,0:T(8,128)} fusion(bf16[1280,1280]{1,0:T(8,128)(2,1)} %copy-done.1, bf16[1024,1280]{1,0:T(8,128)(2,1)} %all-gather.8.cloned.1.call-done), kind=kOutput, calls=%fused_computation.6 | convolution fusion | flops 3355443200 | bytes 11141120 | tf_op jit(solution)/shard_map/dot_general | solution.py:19
  370.6 47.0 %all-gather.6.cloned.1.call-done = bf16[1024,1280]{1,0:T(8,128)(2,1)} async-done(((bf16[64,1280]{1,0:T(8,128)(2,1)}), bf16[1024,1280]{1,0:T(8,128)(2,1)}) %all-gather.6.cloned.1.call-update) | async-done | bytes 2621456 | tf_op jit(solution)/shard_map/all_gather | solution.py:41
  417.7 7.6 %fusion.21 = f32[1024,1280]{1,0:T(8,128)} fusion(bf16[1024,1280]{1,0:T(8,128)(2,1)} %all-gather.6.cloned.1.call-done, bf16[1280,1280]{1,0:T(8,128)(2,1)S(1)} %copy-done), kind=kOutput, calls=%fused_computation.37 | convolution fusion | flops 3355443200 | bytes 11141120 | tf_op jit(solution)/shard_map/dot_general | solution.py:19
  425.2 9.2 %pad_maximum_fusion = f32[1024,2560]{1,0:T(8,128)} fusion(f32[1024,1280]{1,0:T(8,128)} %convolution_bitcast_fusion, f32[1024,1280]{1,0:T(8,128)} %fusion.21), kind=kLoop, calls=%fused_computation | loop fusion | flops 2621440 | bytes 20971520 | tf_op jit(solution)/shard_map/concatenate | solution.py:61
  434.5 0.0 reduce-scatter.2.cloned.1.call-update
  434.5 4.0 copy.6
  438.5 219.7 %reduce-scatter.2.cloned.1.call-done = f32[64,2560]{1,0:T(8,128)} async-done(((f32[1024,2560]{1,0:T(8,128)}), f32[64,2560]{1,0:T(8,128)}) %reduce-scatter.2.cloned.1.call-update) | async-done | bytes 655376 | tf_op jit(solution)/shard_map/reduce_scatter | solution.py:60
  658.3 2.3 fusion.17
  660.6 37.7 %psum.15 = f32[64]{0:T(128)S(1)} all-reduce(f32[64]{0:T(128)S(1)} %add_subtract_fusion), channel_id=1, replica_groups=mesh['row'=16,'col'=16] {'row'}, use_global_device_ids=true, to_apply=%region_5.6 | all-reduce | flops 64 | bytes 512 | tf_op jit(solution)/shard_map/psum | solution.py:72
  698.3 0.5 broadcast_multiply_fusion
  (3 shorter events, 0.0 us)
Async XLA Ops:
  7.2 124.4 %all-gather.4.cloned.1.call-start = ((), (), s32[]{:S(2)}) async-start(), calls=%async_computation.1 | async-start | bytes 5570560 | tf_op jit(solution)/shard_map/all_gather | solution.py:31
  7.9 296.6 %all-reduce.2.cloned.1.call-start = ((), (), s32[]{:S(2)}) async-start(), calls=%async_computation.2 | async-start | bytes 10485760 | tf_op jit(solution)/shard_map/psum | solution.py:15
  134.3 1.9 copy-start
  134.3 227.6 %all-gather.8.cloned.1.call-start = ((), (), s32[]{:S(2)}) async-start(), calls=%async_computation.4 | async-start | bytes 2785280 | tf_op jit(solution)/shard_map/all_gather | solution.py:42
  136.9 280.7 %all-gather.6.cloned.1.call-start = ((), (), s32[]{:S(2)}) async-start(), calls=%async_computation.3 | async-start | bytes 2785280 | tf_op jit(solution)/shard_map/all_gather | solution.py:41
  315.8 1.7 copy-start.1
  318.2 340.1 %reduce-scatter.2.cloned.1.call-start = ((), (), s32[]{:S(2)}) async-start(), calls=%async_computation.5 | async-start | bytes 11141120 | tf_op jit(solution)/shard_map/reduce_scatter | solution.py:60
Sparse Core Ops, SparseCore 0:
  9.8 121.7 all-gather.3
  134.5 169.9 all-reduce.1
  307.8 54.0 all-gather.7
  364.6 53.0 all-gather.5
  434.6 223.6 reduce-scatter.1
where the time goes:
time: 706 us; the launch traced here: 705 us
  waiting for transfers between devices  602 us (85%)
  blocking collectives  37.7 us (5%)
  matrix products  27.5 us (4%)
  other arithmetic  14.8 us (2%)
  between operations  13.8 us (2%)
  local copies, waits for them, and re-layouts  8.93 us (1%)
    reduce_scatter x1, waiting for transfers between devices, per_device(): lax.psum_scatter(jnp.concatenate([contract(cov_rows, omega_prior), contra...  220 us
    psum x1, waiting for transfers between devices, broadcast(): return lax.psum(kept, axis)  167 us
    all_gather x1, waiting for transfers between devices, per_device(): own_slab = lax.all_gather(cell_batch, 'col', axis=0, tiled=True)  124 us
    all_gather x1, waiting for transfers between devices, per_device(): lax.all_gather(cov_updated[:PW], 'row', axis=0, tiled=True)  47 us
    all_gather x1, waiting for transfers between devices, per_device(): lax.all_gather(omega_prior[:PW], 'row', axis=0, tiled=True)  43.7 us
    psum x1, blocking collectives, per_device(): column_objective = lax.psum(quadratic + lasso - logs, 'row') / P_SIZE  37.7 us
    dot_general x2, matrix products, contract(): lax.dot_general(left_rows, right_rows, (((1,), (1,)), ((), ())), preferre...  16.2 us
  transfers between devices with their start and end apart: 5, of which 5 were waited for; matrix products, arithmetic and copies ran while one was open for 4% of the time, Pallas kernels for 0%

commit v1 on v0

--- a/solution.py
+++ b/solution.py
@@ -8,6 +8,18 @@
 decay_weight = 0.5
 step_size = 0.2
 penalty = 1.0
+
+
+def expand_patch(x0, shard_axis):
+    return jnp.concatenate(
+        lax.all_to_all(
+            jnp.stack([x0 for _ in range(lax.psum(1, shard_axis))]),
+            shard_axis,
+            split_axis=0,
+            concat_axis=0,
+        ),
+        axis=0,
+    )
 
 
 def broadcast(value, axis, source):
@@ -28,7 +40,7 @@
     row_width = omega_prior.shape[0]
     col_number = lax.axis_index("col")
     row_number = lax.axis_index("row")
-    own_slab = lax.all_gather(cell_batch, "col", axis=0, tiled=True)
+    own_slab = expand_patch(cell_batch, "col")
     mirrored = broadcast(own_slab, "row", col_number * fold_ratio + 0)
     product = lax.dot_general(
         own_slab, mirrored, (((0,), (0,)), ((), ())), preferred_element_type=jnp.float32

time: 706 us -> 715 us (1.013)
  starting transfers between devices: 0.2 us -> 9.68 us
    all_gather x1 -> x0, waiting for transfers between devices: 124 us -> none  [per_device(): own_slab = lax.all_gather(cell_batch, 'col', axis=0, tiled=True)]
    all_to_all x0 -> x1, waiting for transfers between devices: none -> 119 us  [expand_patch(): lax.all_to_all(jnp.stack([x0 for _ in range(lax.psum(1, shard_axis))]), s...]
    all_to_all x0 -> x1, starting transfers between devices: none -> 9.51 us  [expand_patch(): lax.all_to_all(jnp.stack([x0 for _ in range(lax.psum(1, shard_axis))]), s...]
where the time goes in v1:
time: 715 us
  waiting for transfers between devices  596 us (83%)
  blocking collectives  37.7 us (5%)
  matrix products  27.5 us (4%)
  other arithmetic  17.3 us (2%)
  between operations  13.8 us (2%)
  local copies, waits for them, and re-layouts  12.7 us (2%)
  starting transfers between devices  9.68 us (1%)
    reduce_scatter x1, waiting for transfers between devices, per_device(): lax.psum_scatter(jnp.concatenate([contract(cov_rows, omega_prior), contra...  220 us
    psum x1, waiting for transfers between devices, broadcast(): return lax.psum(kept, axis)  167 us
    all_to_all x1, waiting for transfers between devices, expand_patch(): lax.all_to_all(jnp.stack([x0 for _ in range(lax.psum(1, shard_axis))]), s...  119 us
    all_gather x1, waiting for transfers between devices, per_device(): lax.all_gather(cov_updated[:PW], 'row', axis=0, tiled=True)  47.2 us
    all_gather x1, waiting for transfers between devices, per_device(): lax.all_gather(omega_prior[:PW], 'row', axis=0, tiled=True)  43.7 us
    psum x1, blocking collectives, per_device(): column_objective = lax.psum(quadratic + lasso - logs, 'row') / P_SIZE  37.7 us
    dot_general x2, matrix products, contract(): lax.dot_general(left_rows, right_rows, (((1,), (1,)), ((), ())), preferre...  16.2 us
  transfers between devices with their start and end apart: 5, of which 5 were waited for; matrix products, arithmetic and copies ran while one was open for 4% of the time, Pallas kernels for 0%

profile of v1, /device:TPU:32, one launch (start us, length us, event | category | flops | bytes accessed | tf_op | source)
XLA Modules:
  0.0 714.8 jit_solution(11586458155309151134)
XLA Ops:
  7.2 3.8 stack.2
  11.0 9.5 %all-to-all-start = ((bf16[16,128,1280]{2,1,0:T(8,128)(2,1)}), bf16[16,128,1280]{2,1,0:T(8,128)(2,1)}, u32[]{:S(2)}, u32[]{:S(2)}) async-start(bf16[16,128,1280]{2,1,0:T(8,128)(2,1)} %stack.2), calls=%async_computation | async-start | bytes 10485760 | tf_op jit(solution)/shard_map/all_to_all | solution.py:15
  20.5 0.0 all-reduce.2.cloned.1.call-start
  20.6 118.8 %all-to-all-done = bf16[16,128,1280]{2,1,0:T(8,128)(2,1)} async-done(((bf16[16,128,1280]{2,1,0:T(8,128)(2,1)}), bf16[16,128,1280]{2,1,0:T(8,128)(2,1)}, u32[]{:S(2)}, u32[]{:S(2)}) %all-to-all-start) | async-done | bytes 5242912 | tf_op jit(solution)/shard_map/all_to_all | solution.py:15
  139.4 5.2 broadcast_select_fusion
  144.6 0.0 copy-start
  144.6 0.0 all-reduce.2.cloned.1.call-update
  144.6 0.0 all-gather.5.cloned.1.call-start
  144.6 1.9 copy-done
  146.5 0.7 slice.17
  147.2 0.0 all-gather.5.cloned.1.call-update
  147.2 0.0 all-gather.3.cloned.1.call-start
  147.2 166.6 %all-reduce.2.cloned.1.call-done = bf16[2048,1280]{1,0:T(8,128)(2,1)} async-done(((bf16[2048,1280]{1,0:T(8,128)(2,1)}), bf16[2048,1280]{1,0:T(8,128)(2,1)}) %all-reduce.2.cloned.1.call-update) | async-done | bytes 5242896 | tf_op jit(solution)/shard_map/psum | solution.py:27
  313.8 11.3 %fusion.2 = bf16[1280,1280]{1,0:T(8,128)(2,1)S(1)} fusion(bf16[2048,1280]{1,0:T(8,128)(2,1)} %all-reduce.2.cloned.1.call-done, bf16[2048,1280]{1,0:T(8,128)(2,1)} %bitcast, bf16[1280,1280]{1,0:T(8,128)(2,1)} %param.4), kind=kOutput, calls=%fused_computation.4 | convolution fusion | flops 6719078400 | bytes 17039360 | tf_op jit(solution)/shard_map/dot_general | solution.py:45
  325.1 0.0 copy-start.1
  325.1 1.7 copy-done.1
  326.8 0.7 slice.21
  327.4 0.0 all-gather.3.cloned.1.call-update
  327.5 0.0 reduce-scatter.2.cloned.1.call-start
  327.5 43.7 %all-gather.5.cloned.1.call-done = bf16[1024,1280]{1,0:T(8,128)(2,1)} async-done(((bf16[64,1280]{1,0:T(8,128)(2,1)}), bf16[1024,1280]{1,0:T(8,128)(2,1)}) %all-gather.5.cloned.1.call-update) | async-done | bytes 2621456 | tf_op jit(solution)/shard_map/all_gather | solution.py:54
  371.3 8.7 %convolution_bitcast_fusion = f32[1024,1280]{1,0:T(8,128)} fusion(bf16[1280,1280]{1,0:T(8,128)(2,1)} %copy-done.1, bf16[1024,1280]{1,0:T(8,128)(2,1)} %all-gather.5.cloned.1.call-done), kind=kOutput, calls=%fused_computation.6 | convolution fusion | flops 3355443200 | bytes 11141120 | tf_op jit(solution)/shard_map/dot_general | solution.py:31
  379.9 47.2 %all-gather.3.cloned.1.call-done = bf16[1024,1280]{1,0:T(8,128)(2,1)} async-done(((bf16[64,1280]{1,0:T(8,128)(2,1)}), bf16[1024,1280]{1,0:T(8,128)(2,1)}) %all-gather.3.cloned.1.call-update) | async-done | bytes 2621456 | tf_op jit(solution)/shard_map/all_gather | solution.py:53
  427.1 7.6 %fusion.21 = f32[1024,1280]{1,0:T(8,128)} fusion(bf16[1024,1280]{1,0:T(8,128)(2,1)} %all-gather.3.cloned.1.call-done, bf16[1280,1280]{1,0:T(8,128)(2,1)S(1)} %copy-done), kind=kOutput, calls=%fused_computation.37 | convolution fusion | flops 3355443200 | bytes 11141120 | tf_op jit(solution)/shard_map/dot_general | solution.py:31
  434.7 9.2 %pad_maximum_fusion = f32[1024,2560]{1,0:T(8,128)} fusion(f32[1024,1280]{1,0:T(8,128)} %convolution_bitcast_fusion, f32[1024,1280]{1,0:T(8,128)} %fusion.21), kind=kLoop, calls=%fused_computation | loop fusion | flops 2621440 | bytes 20971520 | tf_op jit(solution)/shard_map/concatenate | solution.py:73
  443.9 0.0 reduce-scatter.2.cloned.1.call-update
  443.9 4.0 copy.6
  448.0 219.7 %reduce-scatter.2.cloned.1.call-done = f32[64,2560]{1,0:T(8,128)} async-done(((f32[1024,2560]{1,0:T(8,128)}), f32[64,2560]{1,0:T(8,128)}) %reduce-scatter.2.cloned.1.call-update) | async-done | bytes 655376 | tf_op jit(solution)/shard_map/reduce_scatter | solution.py:72
  667.7 2.3 fusion.17
  670.0 37.7 %psum.15 = f32[64]{0:T(128)S(1)} all-reduce(f32[64]{0:T(128)S(1)} %add_subtract_fusion), channel_id=1, replica_groups=mesh['row'=16,'col'=16] {'row'}, use_global_device_ids=true, to_apply=%region_5.6 | all-reduce | flops 64 | bytes 512 | tf_op jit(solution)/shard_map/psum | solution.py:84
  707.8 0.5 broadcast_multiply_fusion
  (3 shorter events, 0.0 us)
Async XLA Ops:
  11.0 128.4 %all-to-all-start = ((bf16[16,128,1280]{2,1,0:T(8,128)(2,1)}), bf16[16,128,1280]{2,1,0:T(8,128)(2,1)}, u32[]{:S(2)}, u32[]{:S(2)}) async-start(bf16[16,128,1280]{2,1,0:T(8,128)(2,1)} %stack.2), calls=%async_computation | async-start | bytes 10485760 | tf_op jit(solution)/shard_map/all_to_all | solution.py:15
  20.5 293.3 %all-reduce.2.cloned.1.call-start = ((), (), s32[]{:S(2)}) async-start(), calls=%async_computation.2 | async-start | bytes 10485760 | tf_op jit(solution)/shard_map/psum | solution.py:27
  144.6 1.9 copy-start
  144.6 226.7 %all-gather.5.cloned.1.call-start = ((), (), s32[]{:S(2)}) async-start(), calls=%async_computation.4 | async-start | bytes 2785280 | tf_op jit(solution)/shard_map/all_gather | solution.py:54
  147.2 279.9 %all-gather.3.cloned.1.call-start = ((), (), s32[]{:S(2)}) async-start(), calls=%async_computation.3 | async-start | bytes 2785280 | tf_op jit(solution)/shard_map/all_gather | solution.py:53
  325.1 1.7 copy-start.1
  327.5 340.2 %reduce-scatter.2.cloned.1.call-start = ((), (), s32[]{:S(2)}) async-start(), calls=%async_computation.5 | async-start | bytes 11141120 | tf_op jit(solution)/shard_map/reduce_scatter | solution.py:72
Sparse Core Ops, SparseCore 0:
  144.7 169.0 all-reduce.1
  317.1 54.0 all-gather.4
  374.0 53.0 all-gather.2
  444.0 223.6 reduce-scatter.1
